TPU v7x, 32 devices: a whole 2x2x4 slice. The times are simulated.
32 devices in a mesh: groups: 2 (over y), ctx: 4 (over z), heads: 4 (over x, core).
Axes of the slice: x: 2, y: 2, z: 4, core: 2. Of those that a mesh axis runs over, the one named last changes fastest.
Arguments:
- queries: bfloat16 [2048, 4096], P(('groups', 'ctx'), 'heads'), parts along dimension 0
- keys: bfloat16 [2048, 1024], P(('groups', 'ctx'), 'heads'), parts along dimension 0
- values: bfloat16 [2048, 1024], P(('groups', 'ctx'), 'heads'), parts along dimension 0, may hold values from -6 to 6
- conv_kernel: float32 [32, 6, 11], P('heads')
- head_mix: float32 [8, 4, 4], P('heads')
- norm_gain: float32 [4096], P('heads'), may hold values from 0.5 to 1.5
- bounds: int32 [4], P('groups'), parts along dimension 0, may hold values from 0 to 1024, as said below
Outputs:
- attended: bfloat16 [2048, 4096], P(('groups', 'ctx'), 'heads'), parts along dimension 0
There are 2 independent parts, one for each index of `groups`. A program takes and returns all parts, laid end to end along the dimension named above; an argument that names none is the same for every part. Nothing has to cross between parts.
Inputs may be any that keep to these rules, and one draw needn't show every extreme that they name: bounds[0] < bounds[1], and bounds[1] >= 512.
All inputs are finite; a program needn't handle non-finite values.
Results may differ from a plain program's by a relative error of at most 0.0045.
Values may be sent and summed in bfloat16 or wider, within the bound.
No kernel may reach another device: no remote copies, remote signals or barrier semaphores. Data moves between devices by JAX's collectives and lax.ppermute only.
A program may use at most 64 MiB of HBM per device.

v0:
```python
import jax
import jax.numpy as jnp
from jax import lax
from jax.sharding import PartitionSpec as P

NEG_FILL = -1e30
EPSILON = 1e-06


def from_behind(value, axis, steps):
    count = lax.axis_size(axis)
    leading, last = (max(0, -steps), min(count, count - steps))
    return lax.ppermute(value, axis, [(source, source + steps) for source in range(leading, last)])


def conv_scores(zeroed, kernel, out_rows, out_cols, q_edge, k_edge):
    summed = jnp.zeros(zeroed.shape[:2] + (out_rows, out_cols), jnp.float32)
    for tap_row in range(kernel.shape[2]):
        for tap_col in range(kernel.shape[3]):
            summed = (
                summed
                + kernel[:, :, tap_row, tap_col][:, :, None, None]
                * zeroed[
                    :,
                    :,
                    q_edge - tap_row : q_edge - tap_row + out_rows,
                    2 * k_edge - tap_col : 2 * k_edge - tap_col + out_cols,
                ]
            )
    return summed


def per_device(queries, keys, values, conv_kernel, head_mix, norm_gain, bounds):
    num_rows = queries.shape[0]
    kv_local = head_mix.shape[0]
    heads_per_group = head_mix.shape[1]
    head_width = keys.shape[1] // kv_local
    q_taps = conv_kernel.shape[1]
    k_taps = conv_kernel.shape[2]
    q_edge = q_taps - 1
    k_edge = k_taps // 2
    score_scale = head_width ** (-0.5)
    ctx_size = lax.axis_size("ctx")
    row_first = lax.axis_index("ctx") * num_rows
    start_row = bounds[0]
    end_row = bounds[1]
    prior_rows = from_behind(queries[num_rows - q_edge :], "ctx", 1)
    query_ext = jnp.concatenate([prior_rows, queries], 0).reshape(
        num_rows + q_edge, kv_local, heads_per_group, head_width
    )
    kernel = conv_kernel.reshape(kv_local, heads_per_group, q_taps, k_taps)
    seg_rows = query_ext.shape[0] - q_edge
    ext_pos = row_first - q_edge + jnp.arange(seg_rows + q_edge, dtype=jnp.int32)
    pos = row_first + jnp.arange(seg_rows, dtype=jnp.int32)
    live = (pos >= start_row) & (pos < end_row)
    segments = ((query_ext, ext_pos, pos, live),)

    def attend(carry_state, segment, key_block, value_block, key_first):
        seg_queries, row_ext_pos, row_pos, row_live = segment
        seg_rows = row_pos.shape[0]
        run_max, run_sum, run_acc = carry_state
        key_count = value_block.shape[0]
        raw_scores = (
            jnp.einsum("rgmd,kgd->gmrk", seg_queries, key_block, preferred_element_type=jnp.float32)
            * score_scale
        )
        key_ext_pos = key_first - k_edge + jnp.arange(key_count + 2 * k_edge, dtype=jnp.int32)
        zeroed = jnp.where(key_ext_pos[None, :] <= row_ext_pos[:, None], raw_scores, 0.0)
        mixed_scores = conv_scores(zeroed, kernel, seg_rows, key_count, q_edge, k_edge)
        key_pos = key_first + jnp.arange(key_count, dtype=jnp.int32)
        valid_mask = (key_pos[None, :] <= row_pos[:, None]) & row_live[:, None]
        block_max = jnp.max(jnp.where(valid_mask, mixed_scores, NEG_FILL), axis=-1)
        new_max = jnp.maximum(run_max, block_max)
        weights = jnp.where(valid_mask, jnp.exp(mixed_scores - new_max[..., None]), 0.0)
        factor = jnp.exp(run_max - new_max)
        new_sum = run_sum * factor + jnp.sum(weights, axis=-1)
        product = jnp.einsum(
            "gmrk,kgd->rgmd",
            weights.astype(jnp.bfloat16),
            value_block,
            preferred_element_type=jnp.float32,
        )
        new_acc = run_acc * jnp.transpose(factor, (2, 0, 1))[..., None] + product
        return (new_max, new_sum, new_acc)

    def guarded(carry_state, segment, key_block, value_block, key_first):
        return attend(carry_state, segment, key_block, value_block, key_first)

    def guarded_all(states, key_block, value_block, key_first):
        return tuple(
            (
                guarded(states[idx], segments[idx], key_block, value_block, key_first)
                for idx in range(len(segments))
            )
        )

    def fresh_state(segment):
        seg_rows = segment[2].shape[0]
        return (
            jnp.full((kv_local, heads_per_group, seg_rows), NEG_FILL, jnp.float32),
            jnp.zeros((kv_local, heads_per_group, seg_rows), jnp.float32),
            jnp.zeros((seg_rows, kv_local, heads_per_group, head_width), jnp.float32),
        )

    initial = tuple((fresh_state(segment) for segment in segments))
    boundary = jnp.concatenate([keys[:k_edge], keys[num_rows - k_edge :]], 0)
    edge_table = lax.all_gather(boundary, "ctx", axis=0, tiled=True)
    edge_table = edge_table.reshape(ctx_size, 2 * k_edge, kv_local * head_width)
    blank_rows = jnp.zeros((1, 2 * k_edge, kv_local * head_width), keys.dtype)
    padded_table = jnp.concatenate([blank_rows, edge_table, blank_rows], 0)
    key_piece = lax.all_gather(keys, "ctx", axis=0, tiled=True)
    value_piece = lax.all_gather(values, "ctx", axis=0, tiled=True)
    shards = key_piece.shape[0] // num_rows
    key_split = key_piece.reshape(shards, num_rows, kv_local, head_width)
    value_split = value_piece.reshape(shards, num_rows, kv_local, head_width)

    def per_shard(shard_pos, inner_state):
        lower_edge = lax.dynamic_index_in_dim(padded_table, shard_pos, 0, keepdims=False)[k_edge:]
        upper_edge = lax.dynamic_index_in_dim(padded_table, shard_pos + 2, 0, keepdims=False)[
            :k_edge
        ]
        middle_keys = lax.dynamic_index_in_dim(key_split, shard_pos, 0, keepdims=False)
        block_keys = jnp.concatenate(
            [
                lower_edge.reshape(k_edge, kv_local, head_width),
                middle_keys,
                upper_edge.reshape(k_edge, kv_local, head_width),
            ],
            0,
        )
        block_values = lax.dynamic_index_in_dim(value_split, shard_pos, 0, keepdims=False)
        return guarded_all(inner_state, block_keys, block_values, shard_pos * num_rows)

    final_states = lax.fori_loop(0, shards, per_shard, initial)
    run_max, run_sum, run_acc = final_states[0]
    row_live = segments[0][3]
    seg_rows = row_live.shape[0]
    divisor = jnp.where(row_live[None, None, :], run_sum, 1.0)
    probs_out = run_acc / jnp.transpose(divisor, (2, 0, 1))[..., None]
    blended = jnp.einsum("gab,rgbd->rgad", head_mix, probs_out, precision=lax.Precision.HIGHEST)
    mean_sq = jnp.mean(blended * blended, axis=-1, keepdims=True)
    normed = (
        blended
        * lax.rsqrt(mean_sq + EPSILON)
        * norm_gain.reshape(kv_local, heads_per_group, head_width)
    )
    result = jnp.where(row_live[:, None, None, None], normed, 0.0)
    return result.reshape(seg_rows, kv_local * heads_per_group * head_width).astype(jnp.bfloat16)


def solution(mesh):
    return jax.shard_map(
        per_device,
        mesh=mesh,
        in_specs=(
            P(("groups", "ctx"), "heads"),
            P(("groups", "ctx"), "heads"),
            P(("groups", "ctx"), "heads"),
            P("heads", None, None),
            P("heads", None, None),
            P("heads"),
            P("groups"),
        ),
        out_specs=P(("groups", "ctx"), "heads"),
        check_vma=False,
    )
```

profile of v0, /device:TPU:0, one launch (start us, length us, event | category | flops | bytes accessed | tf_op | source)
XLA Modules:
  0.0 266.3 jit_solution(12256957341839974469)
XLA Ops:
  0.8 4.9 %collective-permute-start = (bf16[5,1024]{1,0:T(8,128)(2,1)S(1)}, bf16[5,1024]{1,0:T(8,128)(2,1)S(1)}, u32[]{:S(2)}, u32[]{:S(2)}) collective-permute-start(bf16[5,1024]{1,0:T(8,128)(2,1)S(1)} %slice.1361), channel_id=1, source_target_pairs={{0,4},{4,8},{8,12},{1,5},{5,9},{9,13},{2,6},{6,10},{10,14},{3,7},{... | collective-permute-start | bytes 30728 | tf_op jit(solution)/shard_map/ppermute | solution.py:13
  6.5 16.0 %all_gather.10 = bf16[1024,256]{1,0:T(8,128)(2,1)S(1)} all-gather(bf16[256,256]{1,0:T(8,128)(2,1)} %param.10), channel_id=1, replica_groups=mesh['groups'=2,'ctx'=4,'heads'=4] {'ctx'}, dimensions={0}, use_global_device_ids=true | all-gather | bytes 655360 | tf_op jit(solution)/shard_map/all_gather | solution.py:111
  22.4 13.1 %all-gather = bf16[4,10,256]{2,1,0:T(8,128)(2,1)S(1)} all-gather(bf16[1,10,256]{2,1,0:T(8,128)(2,1)S(1)} %maximum_bitcast_fusion.2), channel_id=1, replica_groups=mesh['groups'=2,'ctx'=4,'heads'=4] {'ctx'}, dimensions={0}, use_global_device_ids=true | all-gather | bytes 25600 | tf_op jit(solution)/shard_map/all_gather | solution.py:107
  35.6 1.3 fusion.90
  36.9 14.9 %all_gather.11 = bf16[1024,256]{1,0:T(8,128)(2,1)S(1)} all-gather(bf16[256,256]{1,0:T(8,128)(2,1)} %param.11), channel_id=1, replica_groups=mesh['groups'=2,'ctx'=4,'heads'=4] {'ctx'}, dimensions={0}, use_global_device_ids=true | all-gather | bytes 655360 | tf_op jit(solution)/shard_map/all_gather | solution.py:112
  51.8 1.7 compare_and_fusion.2
  56.9 201.9 %while.22 = (s32[]{:T(128)}, f32[2,4,256]{2,1,0:T(4,128)S(1)}, f32[2,4,256]{2,1,0:T(4,128)S(1)}, f32[256,2,4,128]{0,3,2,1:T(8,128)}, f32[2,4,6,11]{1,0,3,2:T(2,1...) while((s32[]{:T(128)}, f32[2,4,256]{2,1,0:T(4,128)S(1)}, ...), condition=%wide.region_3.4_spmd.clone.clone.clone, body=%wide.region_0.3_spmd.clone.clone.clone.sunk | while | flops 351798912 | bytes 160064880 | solution.py:134
  58.9 1.9 bitcast_select_fusion.2
  60.7 1.2 compare_and_fusion.5
  64.7 38.1 %select_reduce_fusion.2 = (f32[2,4,256]{2,1,0:T(4,128)S(1)}, f32[2,4,256,256]{3,2,1,0:T(8,128)}) fusion(pred[256,256]{1,0:T(8,128)(4,1)S(1)} %compare_and_fusion.6, f32[2,4,261,266]{3,2,1,0:T(8,128)S(1)} %bitcast_select_fusion.2, f32[2,4]{1,0:T(2,128)S(1)} %get-tuple-element.735, f32[2,4]{1,0:T(2,128)S(1)} %get-tuple-element.736, ...), kind=kLoop, calls=%fused_computation.136.clone.1 | loop fusion | flops 69728256 | bytes 140585024 | tf_op jit(solution)/shard_map/while/body/eval_jaxpr/reduce_max | solution.py:72
  103.0 3.3 %fusion.106 = f32[256,2,4,128]{0,3,2,1:T(8,128)} fusion(f32[2,4,256,256]{3,2,1,0:T(8,128)} %get-tuple-element.803, f32[256,2,4,128]{0,3,2,1:T(8,128)} %get-tuple-element.829, f32[2,4,256]{2,1,0:T(4,128)S(1)} %get-tuple-element.847, pred[256,256]{1,0:T(8,128)(4,1)S(1)} %compare_and_fusion.6, f32[256,2,4]{0,2,1:T(4,128)S(1)} %get-tuple-element.804, ...), kind=kOutput, calls=%fused_computation.140.clone.1 | convolution fusion | flops 136577024 | bytes 4407297 | tf_op jit(solution)/shard_map/while/body/eval_jaxpr/gmrk,kgd->rgmd/dot_general | solution.py:77
  109.2 1.9 bitcast_select_fusion.2
  111.0 1.2 compare_and_fusion.5
  115.0 38.1 %select_reduce_fusion.2 = (f32[2,4,256]{2,1,0:T(4,128)S(1)}, f32[2,4,256,256]{3,2,1,0:T(8,128)}) fusion(pred[256,256]{1,0:T(8,128)(4,1)S(1)} %compare_and_fusion.6, f32[2,4,261,266]{3,2,1,0:T(8,128)S(1)} %bitcast_select_fusion.2, f32[2,4]{1,0:T(2,128)S(1)} %get-tuple-element.735, f32[2,4]{1,0:T(2,128)S(1)} %get-tuple-element.736, ...), kind=kLoop, calls=%fused_computation.136.clone.1 | loop fusion | flops 69728256 | bytes 140585024 | tf_op jit(solution)/shard_map/while/body/eval_jaxpr/reduce_max | solution.py:72
  153.3 3.6 %fusion.106 = f32[256,2,4,128]{0,3,2,1:T(8,128)} fusion(f32[2,4,256,256]{3,2,1,0:T(8,128)} %get-tuple-element.803, f32[256,2,4,128]{0,3,2,1:T(8,128)} %get-tuple-element.829, f32[2,4,256]{2,1,0:T(4,128)S(1)} %get-tuple-element.847, pred[256,256]{1,0:T(8,128)(4,1)S(1)} %compare_and_fusion.6, f32[256,2,4]{0,2,1:T(4,128)S(1)} %get-tuple-element.804, ...), kind=kOutput, calls=%fused_computation.140.clone.1 | convolution fusion | flops 136577024 | bytes 4407297 | tf_op jit(solution)/shard_map/while/body/eval_jaxpr/gmrk,kgd->rgmd/dot_general | solution.py:77
  159.7 1.9 bitcast_select_fusion.2
  165.6 38.1 %select_reduce_fusion.2 = (f32[2,4,256]{2,1,0:T(4,128)S(1)}, f32[2,4,256,256]{3,2,1,0:T(8,128)}) fusion(pred[256,256]{1,0:T(8,128)(4,1)S(1)} %compare_and_fusion.6, f32[2,4,261,266]{3,2,1,0:T(8,128)S(1)} %bitcast_select_fusion.2, f32[2,4]{1,0:T(2,128)S(1)} %get-tuple-element.735, f32[2,4]{1,0:T(2,128)S(1)} %get-tuple-element.736, ...), kind=kLoop, calls=%fused_computation.136.clone.1 | loop fusion | flops 69728256 | bytes 140585024 | tf_op jit(solution)/shard_map/while/body/eval_jaxpr/reduce_max | solution.py:72
  203.8 3.6 %fusion.106 = f32[256,2,4,128]{0,3,2,1:T(8,128)} fusion(f32[2,4,256,256]{3,2,1,0:T(8,128)} %get-tuple-element.803, f32[256,2,4,128]{0,3,2,1:T(8,128)} %get-tuple-element.829, f32[2,4,256]{2,1,0:T(4,128)S(1)} %get-tuple-element.847, pred[256,256]{1,0:T(8,128)(4,1)S(1)} %compare_and_fusion.6, f32[256,2,4]{0,2,1:T(4,128)S(1)} %get-tuple-element.804, ...), kind=kOutput, calls=%fused_computation.140.clone.1 | convolution fusion | flops 136577024 | bytes 4407297 | tf_op jit(solution)/shard_map/while/body/eval_jaxpr/gmrk,kgd->rgmd/dot_general | solution.py:77
  210.3 1.9 bitcast_select_fusion.2
  216.1 38.1 %select_reduce_fusion.2 = (f32[2,4,256]{2,1,0:T(4,128)S(1)}, f32[2,4,256,256]{3,2,1,0:T(8,128)}) fusion(pred[256,256]{1,0:T(8,128)(4,1)S(1)} %compare_and_fusion.6, f32[2,4,261,266]{3,2,1,0:T(8,128)S(1)} %bitcast_select_fusion.2, f32[2,4]{1,0:T(2,128)S(1)} %get-tuple-element.735, f32[2,4]{1,0:T(2,128)S(1)} %get-tuple-element.736, ...), kind=kLoop, calls=%fused_computation.136.clone.1 | loop fusion | flops 69728256 | bytes 140585024 | tf_op jit(solution)/shard_map/while/body/eval_jaxpr/reduce_max | solution.py:72
  254.4 3.6 %fusion.106 = f32[256,2,4,128]{0,3,2,1:T(8,128)} fusion(f32[2,4,256,256]{3,2,1,0:T(8,128)} %get-tuple-element.803, f32[256,2,4,128]{0,3,2,1:T(8,128)} %get-tuple-element.829, f32[2,4,256]{2,1,0:T(4,128)S(1)} %get-tuple-element.847, pred[256,256]{1,0:T(8,128)(4,1)S(1)} %compare_and_fusion.6, f32[256,2,4]{0,2,1:T(4,128)S(1)} %get-tuple-element.804, ...), kind=kOutput, calls=%fused_computation.140.clone.1 | convolution fusion | flops 136577024 | bytes 4407297 | tf_op jit(solution)/shard_map/while/body/eval_jaxpr/gmrk,kgd->rgmd/dot_general | solution.py:77
  259.4 1.3 broadcast_divide_fusion
  261.1 2.3 multiply_reduce_fusion
  263.5 1.5 select_convert_fusion
  (124 shorter events, 32.1 us)
Async XLA Ops:
  0.0 261.1 %copy-start = (f32[2,4,4]{2,1,0:T(4,128)S(1)}, f32[2,4,4]{2,1,0:T(4,128)}, u32[]{:S(2)}) copy-start(f32[2,4,4]{2,1,0:T(4,128)} %param.13) | copy-start | bytes 388
  0.0 55.5 %copy-start.2 = (bf16[256,1024]{1,0:T(8,128)(2,1)S(1)}, bf16[256,1024]{1,0:T(8,128)(2,1)}, u32[]{:S(2)}) copy-start(bf16[256,1024]{1,0:T(8,128)(2,1)} %param.9) | copy-start | bytes 1572868
  0.0 55.4 %copy-start.5 = (f32[8,6,11]{2,0,1:T(8,128)S(1)}, f32[8,6,11]{2,0,1:T(8,128)}, u32[]{:S(2)}) copy-start(f32[8,6,11]{2,0,1:T(8,128)} %param.12) | copy-start | bytes 6340
  0.8 54.7 %collective-permute-start = (bf16[5,1024]{1,0:T(8,128)(2,1)S(1)}, bf16[5,1024]{1,0:T(8,128)(2,1)S(1)}, u32[]{:S(2)}, u32[]{:S(2)}) collective-permute-start(bf16[5,1024]{1,0:T(8,128)(2,1)S(1)} %slice.1361), channel_id=1, source_target_pairs={{0,4},{4,8},{8,12},{1,5},{5,9},{9,13},{2,6},{6,10},{10,14},{3,7},{... | collective-permute-start | bytes 30728 | tf_op jit(solution)/shard_map/ppermute | solution.py:13
  56.9 2.0 copy-start.3
  103.0 3.4 %copy-start.1 = (f32[2,4,256,256]{3,2,1,0:T(8,128)S(1)}, f32[2,4,256,256]{3,2,1,0:T(8,128)}, u32[]{:S(2)}) copy-start(f32[2,4,256,256]{3,2,1,0:T(8,128)} %get-tuple-element.803) | copy-start | bytes 6291460 | tf_op jit(solution)/shard_map/while
  106.3 0.8 copy-start.4
  107.1 2.0 copy-start.3
  153.3 3.6 %copy-start.1 = (f32[2,4,256,256]{3,2,1,0:T(8,128)S(1)}, f32[2,4,256,256]{3,2,1,0:T(8,128)}, u32[]{:S(2)}) copy-start(f32[2,4,256,256]{3,2,1,0:T(8,128)} %get-tuple-element.803) | copy-start | bytes 6291460 | tf_op jit(solution)/shard_map/while
  156.9 0.8 copy-start.4
  157.7 2.0 copy-start.3
  203.8 3.6 %copy-start.1 = (f32[2,4,256,256]{3,2,1,0:T(8,128)S(1)}, f32[2,4,256,256]{3,2,1,0:T(8,128)}, u32[]{:S(2)}) copy-start(f32[2,4,256,256]{3,2,1,0:T(8,128)} %get-tuple-element.803) | copy-start | bytes 6291460 | tf_op jit(solution)/shard_map/while
  207.4 0.8 copy-start.4
  208.2 2.0 copy-start.3
  254.4 3.6 %copy-start.1 = (f32[2,4,256,256]{3,2,1,0:T(8,128)S(1)}, f32[2,4,256,256]{3,2,1,0:T(8,128)}, u32[]{:S(2)}) copy-start(f32[2,4,256,256]{3,2,1,0:T(8,128)} %get-tuple-element.803) | copy-start | bytes 6291460 | tf_op jit(solution)/shard_map/while
  258.0 0.8 copy-start.4
  260.7 2.8 %copy-start.6 = (pred[256]{0:T(512)(128)(4,1)S(1)}, pred[256]{0:T(512)(128)(4,1)}, u32[]{:S(2)}) copy-start(pred[256]{0:T(512)(128)(4,1)} %compare_and_fusion.2) | copy-start | bytes 772
  260.7 2.8 %copy-start.7 = (f32[1024]{0:T(1024)S(1)}, f32[1024]{0:T(1024)}, u32[]{:S(2)}) copy-start(f32[1024]{0:T(1024)} %param.14) | copy-start | bytes 12292
where the time goes:
time: 267 us; the launch traced here: 266 us
  other arithmetic  167 us (63%)
  blocking collectives  44 us (16%)
  local copies, waits for them, and re-layouts  26 us (10%)
  matrix products  23.9 us (9%)
  starting transfers between devices  4.95 us (2%)
    reduce_max x4, other arithmetic, attend(): block_max = jnp.max(jnp.where(valid_mask, mixed_scores, NEG_FILL), axis=-1)  152 us
    all_gather x1, blocking collectives, per_device(): key_piece = lax.all_gather(keys, 'ctx', axis=0, tiled=True)  16 us
    all_gather x1, blocking collectives, per_device(): value_piece = lax.all_gather(values, 'ctx', axis=0, tiled=True)  14.9 us
    dot_general x4, matrix products, attend(): jnp.einsum('gmrk,kgd->rgmd', weights.astype(jnp.bfloat16), value_block, p...  14.2 us
    all_gather x1, blocking collectives, per_device(): edge_table = lax.all_gather(boundary, 'ctx', axis=0, tiled=True)  13.1 us
    mul x16, local copies, waits for them, and re-layouts, conv_scores(): kernel[:, :, tap_row, tap_col][:, :, None, None]  10.4 us
    dot_general x4, matrix products, attend(): jnp.einsum('rgmd,kgd->gmrk', seg_queries, key_block, preferred_element_ty...  7.42 us
    and x5, other arithmetic, per_device(): live = (pos >= start_row) & (pos < end_row)  6.71 us
  transfers between devices with their start and end apart: 1, of which 0 were waited for; matrix products, arithmetic and copies ran while one was open for 2% of the time, Pallas kernels for 0%

commit v1 on v0

--- a/solution.py
+++ b/solution.py
@@ -109,7 +109,12 @@
     blank_rows = jnp.zeros((1, 2 * k_edge, kv_local * head_width), keys.dtype)
     padded_table = jnp.concatenate([blank_rows, edge_table, blank_rows], 0)
     key_piece = lax.all_gather(keys, "ctx", axis=0, tiled=True)
-    value_piece = lax.all_gather(values, "ctx", axis=0, tiled=True)
+    ring = [values]
+    for hop in range(3):
+        ring.append(lax.ppermute(ring[-1], "ctx", [(dev, (dev + 1) % 4) for dev in range(4)]))
+    value_piece = jnp.roll(
+        jnp.concatenate(ring[::-1], axis=0), (lax.axis_index("ctx") + 1) * ring[0].shape[0], axis=0
+    )
     shards = key_piece.shape[0] // num_rows
     key_split = key_piece.reshape(shards, num_rows, kv_local, head_width)
     value_split = value_piece.reshape(shards, num_rows, kv_local, head_width)

time: 267 us -> 257 us (0.963)
  blocking collectives: 44 us -> 29.2 us
  starting transfers between devices: 4.95 us -> 8.27 us
    all_gather x1 -> x0, blocking collectives: 14.9 us -> none  [per_device(): value_piece = lax.all_gather(values, 'ctx', axis=0, tiled=True)]
    ppermute x0 -> x3, starting transfers between devices: none -> 4.8 us  [per_device(): lax.ppermute(ring[-1], 'ctx', [(dev, (dev + 1) % 4) for dev in range(4)])]
  transfers between devices with their start and end apart: 1 -> 4, of which waited for: 0 -> 1; matrix products, arithmetic and copies ran while one was open for 2% -> 3% of each run, Pallas kernels for 0% -> 0%
where the time goes in v1:
time: 257 us; the launch traced here: 256 us
  other arithmetic  167 us (65%)
  blocking collectives  29.2 us (11%)
  local copies, waits for them, and re-layouts  26.9 us (10%)
  matrix products  23.9 us (9%)
  starting transfers between devices  8.27 us (3%)
    reduce_max x4, other arithmetic, attend(): block_max = jnp.max(jnp.where(valid_mask, mixed_scores, NEG_FILL), axis=-1)  152 us
    all_gather x1, blocking collectives, per_device(): key_piece = lax.all_gather(keys, 'ctx', axis=0, tiled=True)  15.8 us
    dot_general x4, matrix products, attend(): jnp.einsum('gmrk,kgd->rgmd', weights.astype(jnp.bfloat16), value_block, p...  14.2 us
    all_gather x1, blocking collectives, per_device(): edge_table = lax.all_gather(boundary, 'ctx', axis=0, tiled=True)  13.5 us
    mul x16, local copies, waits for them, and re-layouts, conv_scores(): kernel[:, :, tap_row, tap_col][:, :, None, None]  10.4 us
    dot_general x4, matrix products, attend(): jnp.einsum('rgmd,kgd->gmrk', seg_queries, key_block, preferred_element_ty...  7.42 us
    and x5, other arithmetic, per_device(): live = (pos >= start_row) & (pos < end_row)  6.49 us
  transfers between devices with their start and end apart: 4, of which 1 were waited for; matrix products, arithmetic and copies ran while one was open for 3% of the time, Pallas kernels for 0%

profile of v1, /device:TPU:0, one launch (start us, length us, event | category | flops | bytes accessed | tf_op | source)
XLA Modules:
  0.0 255.9 jit_solution(3120452208323088006)
XLA Ops:
  0.0 3.1 %collective-permute-start.1 = (bf16[256,256]{1,0:T(8,128)(2,1)}, bf16[256,256]{1,0:T(8,128)(2,1)S(1)}, u32[]{:S(2)}, u32[]{:S(2)}) collective-permute-start(bf16[256,256]{1,0:T(8,128)(2,1)} %param.11), channel_id=1, source_target_pairs={{0,4},{4,8},{8,12},{12,0},{1,5},{5,9},{9,13},{13,1},{2,6},{6,10},{... | collective-permute-start | bytes 393224 | tf_op jit(solution)/shard_map/ppermute | solution.py:114
  3.8 3.5 %collective-permute-start = (bf16[5,1024]{1,0:T(8,128)(2,1)S(1)}, bf16[5,1024]{1,0:T(8,128)(2,1)S(1)}, u32[]{:S(2)}, u32[]{:S(2)}) collective-permute-start(bf16[5,1024]{1,0:T(8,128)(2,1)S(1)} %slice.1361), channel_id=1, source_target_pairs={{0,4},{4,8},{8,12},{1,5},{5,9},{9,13},{2,6},{6,10},{10,14},{3,7},{... | collective-permute-start | bytes 30728 | tf_op jit(solution)/shard_map/ppermute | solution.py:13
  8.0 15.8 %all_gather.7 = bf16[1024,256]{1,0:T(8,128)(2,1)S(1)} all-gather(bf16[256,256]{1,0:T(8,128)(2,1)} %param.10), channel_id=1, replica_groups=mesh['groups'=2,'ctx'=4,'heads'=4] {'ctx'}, dimensions={0}, use_global_device_ids=true | all-gather | bytes 655360 | tf_op jit(solution)/shard_map/all_gather | solution.py:111
  23.8 1.3 fusion.90
  25.1 13.5 %all-gather = bf16[4,10,256]{2,1,0:T(8,128)(2,1)S(1)} all-gather(bf16[1,10,256]{2,1,0:T(8,128)(2,1)S(1)} %maximum_bitcast_fusion.2), channel_id=1, replica_groups=mesh['groups'=2,'ctx'=4,'heads'=4] {'ctx'}, dimensions={0}, use_global_device_ids=true | all-gather | bytes 25600 | tf_op jit(solution)/shard_map/all_gather | solution.py:107
  38.6 1.7 collective-permute-start.3
  40.3 1.7 compare_and_fusion.2
  46.6 201.7 %while.22 = (s32[]{:T(128)}, f32[2,4,256]{2,1,0:T(4,128)S(1)}, f32[2,4,256]{2,1,0:T(4,128)S(1)}, f32[256,2,4,128]{0,3,2,1:T(8,128)}, f32[2,4,6,11]{1,0,3,2:T(2,1...) while((s32[]{:T(128)}, f32[2,4,256]{2,1,0:T(4,128)S(1)}, ...), condition=%wide.region_3.4_spmd.clone.clone.clone, body=%wide.region_0.3_spmd.clone.clone.clone.sunk | while | flops 351798912 | bytes 160064880 | solution.py:139
  48.6 1.9 bitcast_select_fusion.2
  50.5 1.2 compare_and_fusion.5
  54.4 38.1 %select_reduce_fusion.2 = (f32[2,4,256]{2,1,0:T(4,128)S(1)}, f32[2,4,256,256]{3,2,1,0:T(8,128)}) fusion(pred[256,256]{1,0:T(8,128)(4,1)S(1)} %compare_and_fusion.6, f32[2,4,261,266]{3,2,1,0:T(8,128)S(1)} %bitcast_select_fusion.2, f32[2,4]{1,0:T(2,128)S(1)} %get-tuple-element.735, f32[2,4]{1,0:T(2,128)S(1)} %get-tuple-element.736, ...), kind=kLoop, calls=%fused_computation.136.clone.1 | loop fusion | flops 69728256 | bytes 140585024 | tf_op jit(solution)/shard_map/while/body/eval_jaxpr/reduce_max | solution.py:72
  92.7 3.3 %fusion.106 = f32[256,2,4,128]{0,3,2,1:T(8,128)} fusion(f32[2,4,256,256]{3,2,1,0:T(8,128)} %get-tuple-element.803, f32[256,2,4,128]{0,3,2,1:T(8,128)} %get-tuple-element.829, f32[2,4,256]{2,1,0:T(4,128)S(1)} %get-tuple-element.847, pred[256,256]{1,0:T(8,128)(4,1)S(1)} %compare_and_fusion.6, f32[256,2,4]{0,2,1:T(4,128)S(1)} %get-tuple-element.804, ...), kind=kOutput, calls=%fused_computation.140.clone.1 | convolution fusion | flops 136577024 | bytes 4407297 | tf_op jit(solution)/shard_map/while/body/eval_jaxpr/gmrk,kgd->rgmd/dot_general | solution.py:77
  98.9 1.9 bitcast_select_fusion.2
  104.7 38.1 %select_reduce_fusion.2 = (f32[2,4,256]{2,1,0:T(4,128)S(1)}, f32[2,4,256,256]{3,2,1,0:T(8,128)}) fusion(pred[256,256]{1,0:T(8,128)(4,1)S(1)} %compare_and_fusion.6, f32[2,4,261,266]{3,2,1,0:T(8,128)S(1)} %bitcast_select_fusion.2, f32[2,4]{1,0:T(2,128)S(1)} %get-tuple-element.735, f32[2,4]{1,0:T(2,128)S(1)} %get-tuple-element.736, ...), kind=kLoop, calls=%fused_computation.136.clone.1 | loop fusion | flops 69728256 | bytes 140585024 | tf_op jit(solution)/shard_map/while/body/eval_jaxpr/reduce_max | solution.py:72
  142.9 3.6 %fusion.106 = f32[256,2,4,128]{0,3,2,1:T(8,128)} fusion(f32[2,4,256,256]{3,2,1,0:T(8,128)} %get-tuple-element.803, f32[256,2,4,128]{0,3,2,1:T(8,128)} %get-tuple-element.829, f32[2,4,256]{2,1,0:T(4,128)S(1)} %get-tuple-element.847, pred[256,256]{1,0:T(8,128)(4,1)S(1)} %compare_and_fusion.6, f32[256,2,4]{0,2,1:T(4,128)S(1)} %get-tuple-element.804, ...), kind=kOutput, calls=%fused_computation.140.clone.1 | convolution fusion | flops 136577024 | bytes 4407297 | tf_op jit(solution)/shard_map/while/body/eval_jaxpr/gmrk,kgd->rgmd/dot_general | solution.py:77
  149.4 1.9 bitcast_select_fusion.2
  155.2 38.1 %select_reduce_fusion.2 = (f32[2,4,256]{2,1,0:T(4,128)S(1)}, f32[2,4,256,256]{3,2,1,0:T(8,128)}) fusion(pred[256,256]{1,0:T(8,128)(4,1)S(1)} %compare_and_fusion.6, f32[2,4,261,266]{3,2,1,0:T(8,128)S(1)} %bitcast_select_fusion.2, f32[2,4]{1,0:T(2,128)S(1)} %get-tuple-element.735, f32[2,4]{1,0:T(2,128)S(1)} %get-tuple-element.736, ...), kind=kLoop, calls=%fused_computation.136.clone.1 | loop fusion | flops 69728256 | bytes 140585024 | tf_op jit(solution)/shard_map/while/body/eval_jaxpr/reduce_max | solution.py:72
  193.4 3.6 %fusion.106 = f32[256,2,4,128]{0,3,2,1:T(8,128)} fusion(f32[2,4,256,256]{3,2,1,0:T(8,128)} %get-tuple-element.803, f32[256,2,4,128]{0,3,2,1:T(8,128)} %get-tuple-element.829, f32[2,4,256]{2,1,0:T(4,128)S(1)} %get-tuple-element.847, pred[256,256]{1,0:T(8,128)(4,1)S(1)} %compare_and_fusion.6, f32[256,2,4]{0,2,1:T(4,128)S(1)} %get-tuple-element.804, ...), kind=kOutput, calls=%fused_computation.140.clone.1 | convolution fusion | flops 136577024 | bytes 4407297 | tf_op jit(solution)/shard_map/while/body/eval_jaxpr/gmrk,kgd->rgmd/dot_general | solution.py:77
  199.9 1.9 bitcast_select_fusion.2
  205.7 38.1 %select_reduce_fusion.2 = (f32[2,4,256]{2,1,0:T(4,128)S(1)}, f32[2,4,256,256]{3,2,1,0:T(8,128)}) fusion(pred[256,256]{1,0:T(8,128)(4,1)S(1)} %compare_and_fusion.6, f32[2,4,261,266]{3,2,1,0:T(8,128)S(1)} %bitcast_select_fusion.2, f32[2,4]{1,0:T(2,128)S(1)} %get-tuple-element.735, f32[2,4]{1,0:T(2,128)S(1)} %get-tuple-element.736, ...), kind=kLoop, calls=%fused_computation.136.clone.1 | loop fusion | flops 69728256 | bytes 140585024 | tf_op jit(solution)/shard_map/while/body/eval_jaxpr/reduce_max | solution.py:72
  243.9 3.6 %fusion.106 = f32[256,2,4,128]{0,3,2,1:T(8,128)} fusion(f32[2,4,256,256]{3,2,1,0:T(8,128)} %get-tuple-element.803, f32[256,2,4,128]{0,3,2,1:T(8,128)} %get-tuple-element.829, f32[2,4,256]{2,1,0:T(4,128)S(1)} %get-tuple-element.847, pred[256,256]{1,0:T(8,128)(4,1)S(1)} %compare_and_fusion.6, f32[256,2,4]{0,2,1:T(4,128)S(1)} %get-tuple-element.804, ...), kind=kOutput, calls=%fused_computation.140.clone.1 | convolution fusion | flops 136577024 | bytes 4407297 | tf_op jit(solution)/shard_map/while/body/eval_jaxpr/gmrk,kgd->rgmd/dot_general | solution.py:77
  249.0 1.3 broadcast_divide_fusion
  250.7 2.3 multiply_reduce_fusion
  253.1 1.5 select_convert_fusion
  (138 shorter events, 34.5 us)
Async XLA Ops:
  0.0 250.7 %copy-start = (f32[2,4,4]{2,1,0:T(4,128)S(1)}, f32[2,4,4]{2,1,0:T(4,128)}, u32[]{:S(2)}) copy-start(f32[2,4,4]{2,1,0:T(4,128)} %param.13) | copy-start | bytes 388
  0.0 43.9 %copy-start.2 = (bf16[256,1024]{1,0:T(8,128)(2,1)S(1)}, bf16[256,1024]{1,0:T(8,128)(2,1)}, u32[]{:S(2)}) copy-start(bf16[256,1024]{1,0:T(8,128)(2,1)} %param.9) | copy-start | bytes 1572868
  0.0 23.8 %collective-permute-start.1 = (bf16[256,256]{1,0:T(8,128)(2,1)}, bf16[256,256]{1,0:T(8,128)(2,1)S(1)}, u32[]{:S(2)}, u32[]{:S(2)}) collective-permute-start(bf16[256,256]{1,0:T(8,128)(2,1)} %param.11), channel_id=1, source_target_pairs={{0,4},{4,8},{8,12},{12,0},{1,5},{5,9},{9,13},{13,1},{2,6},{6,10},{... | collective-permute-start | bytes 393224 | tf_op jit(solution)/shard_map/ppermute | solution.py:114
  3.8 40.2 %collective-permute-start = (bf16[5,1024]{1,0:T(8,128)(2,1)S(1)}, bf16[5,1024]{1,0:T(8,128)(2,1)S(1)}, u32[]{:S(2)}, u32[]{:S(2)}) collective-permute-start(bf16[5,1024]{1,0:T(8,128)(2,1)S(1)} %slice.1361), channel_id=1, source_target_pairs={{0,4},{4,8},{8,12},{1,5},{5,9},{9,13},{2,6},{6,10},{10,14},{3,7},{... | collective-permute-start | bytes 30728 | tf_op jit(solution)/shard_map/ppermute | solution.py:13
  23.8 14.9 %collective-permute-start.2 = (bf16[256,256]{1,0:T(8,128)(2,1)S(1)}, bf16[256,256]{1,0:T(8,128)(2,1)S(1)}, u32[]{:S(2)}, u32[]{:S(2)}) collective-permute-start(bf16[256,256]{1,0:T(8,128)(2,1)S(1)} %collective-permute-done.1), channel_id=1, source_target_pairs={{0,4},{4,8},{8,12},{12,0},{1,5},{5,9},{9,13},{13,1},{2,6},{6,10},{... | collective-permute-start | bytes 393224 | tf_op jit(solution)/shard_map/ppermute | solution.py:114
  38.6 6.8 %collective-permute-start.3 = (bf16[256,256]{1,0:T(8,128)(2,1)S(1)}, bf16[256,256]{1,0:T(8,128)(2,1)S(1)}, u32[]{:S(2)}, u32[]{:S(2)}) collective-permute-start(bf16[256,256]{1,0:T(8,128)(2,1)S(1)} %collective-permute-done.2), channel_id=1, source_target_pairs={{0,4},{4,8},{8,12},{12,0},{1,5},{5,9},{9,13},{13,1},{2,6},{6,10},{... | collective-permute-start | bytes 393224 | tf_op jit(solution)/shard_map/ppermute | solution.py:114
  43.0 2.5 copy-start.3
  46.6 2.0 copy-start.4
  92.7 3.4 %copy-start.1 = (f32[2,4,256,256]{3,2,1,0:T(8,128)S(1)}, f32[2,4,256,256]{3,2,1,0:T(8,128)}, u32[]{:S(2)}) copy-start(f32[2,4,256,256]{3,2,1,0:T(8,128)} %get-tuple-element.803) | copy-start | bytes 6291460 | tf_op jit(solution)/shard_map/while
  96.0 0.8 copy-start.5
  96.8 2.0 copy-start.4
  142.9 3.6 %copy-start.1 = (f32[2,4,256,256]{3,2,1,0:T(8,128)S(1)}, f32[2,4,256,256]{3,2,1,0:T(8,128)}, u32[]{:S(2)}) copy-start(f32[2,4,256,256]{3,2,1,0:T(8,128)} %get-tuple-element.803) | copy-start | bytes 6291460 | tf_op jit(solution)/shard_map/while
  146.5 0.8 copy-start.5
  147.3 2.0 copy-start.4
  193.4 3.6 %copy-start.1 = (f32[2,4,256,256]{3,2,1,0:T(8,128)S(1)}, f32[2,4,256,256]{3,2,1,0:T(8,128)}, u32[]{:S(2)}) copy-start(f32[2,4,256,256]{3,2,1,0:T(8,128)} %get-tuple-element.803) | copy-start | bytes 6291460 | tf_op jit(solution)/shard_map/while
  197.0 0.8 copy-start.5
  197.8 2.0 copy-start.4
  243.9 3.6 %copy-start.1 = (f32[2,4,256,256]{3,2,1,0:T(8,128)S(1)}, f32[2,4,256,256]{3,2,1,0:T(8,128)}, u32[]{:S(2)}) copy-start(f32[2,4,256,256]{3,2,1,0:T(8,128)} %get-tuple-element.803) | copy-start | bytes 6291460 | tf_op jit(solution)/shard_map/while
  247.5 0.8 copy-start.5
  250.3 2.8 %copy-start.6 = (pred[256]{0:T(512)(128)(4,1)S(1)}, pred[256]{0:T(512)(128)(4,1)}, u32[]{:S(2)}) copy-start(pred[256]{0:T(512)(128)(4,1)} %compare_and_fusion.2) | copy-start | bytes 772
  250.3 2.8 %copy-start.7 = (f32[1024]{0:T(1024)S(1)}, f32[1024]{0:T(1024)}, u32[]{:S(2)}) copy-start(f32[1024]{0:T(1024)} %param.14) | copy-start | bytes 12292
